TPU v7x, 256 devices: a whole 4x4x8 slice. The times are simulated.
256 devices in a mesh: term: 32 (over z_hi, x, core), sector: 8 (over y, z_lo).
Axes of the slice: x: 4, y: 4, z: 8 (z_hi: 4, z_lo: 2; z = z_hi * 2 + z_lo), core: 2. Of those that a mesh axis runs over, the one named last changes fastest.
Arguments:
- wave: float32 [8, 512, 512], P('sector', 'term'), may hold values from -6 to 6
- left_ops: bfloat16 [256, 8, 512, 512], P('term', 'sector'), may hold values from -1 to 1
- right_ops: bfloat16 [256, 8, 512, 512], P('term', 'sector'), may hold values from -4 to 1
- diagonal: float32 [8, 512, 512], P('sector', 'term'), may hold values from -21 to 0
- block_size: int32 [8], replicated, may hold values from 128 to 512, as said below
- source: int32 [256, 8], P('term'), may hold values from 0 to 7, as said below
Outputs:
- new_vector: float32 [8, 512, 512], P('sector', 'term')
- new_sigma: float32 [8, 512, 512], P('sector', 'term')
- subspace: float32 [2, 2], replicated
Inputs may be any that keep to these rules, and one draw needn't show every extreme that they name: `block_size`: every block size lies between 128 and 512; some sector has exactly 512. `source`: entries name sectors.
All inputs are finite; a program needn't handle non-finite values.
Results may differ from a plain program's by a relative error of at most 0.005.
Values may be sent and summed in bfloat16 or wider, within the bound.
A program may use at most 64 MiB of HBM per device.

v0:
```python
import jax
import jax.numpy as jnp
from jax import lax
from jax.sharding import PartitionSpec as P


def local(wave, left_ops, right_ops, diagonal, block_size, source):
    sec_dev = wave.shape[0]
    slab_rows = wave.shape[1]
    width = wave.shape[2]
    total = float(block_size.shape[0] * width * width)
    first_row = lax.axis_index("term") * slab_rows
    first_sector = lax.axis_index("sector") * sec_dev
    sizes_owned = lax.dynamic_slice_in_dim(block_size, first_sector, sec_dev)
    row_index = first_row + jnp.arange(slab_rows)
    col_index = jnp.arange(width)
    valid = (
        (row_index[None, :, None] < sizes_owned[:, None, None])
        & (col_index[None, None, :] < sizes_owned[:, None, None])
    ).astype(jnp.float32)
    sources = lax.dynamic_slice_in_dim(source, first_sector, sec_dev, 1)
    masked = wave * valid
    squares = lax.psum(jnp.sum(masked * masked), ("term", "sector"))
    first_vec = masked / jnp.sqrt(squares / total + 1e-06)

    def apply_ham(vector):
        vector_b = vector.astype(jnp.bfloat16)
        blocks = lax.all_gather(vector_b, "term", axis=1, tiled=True)
        every_block = lax.all_gather(blocks, "sector", axis=0, tiled=True)
        chosen = jnp.take(every_block, sources, axis=0)
        halfway = jnp.einsum(
            "tpij,tpjk->tpik", left_ops, chosen, preferred_element_type=jnp.float32
        )
        halfway_b = halfway.astype(jnp.bfloat16)
        partial_sum = jnp.einsum(
            "tpij,tpkj->pik", halfway_b, right_ops, preferred_element_type=jnp.float32
        )
        owned = lax.psum_scatter(partial_sum, "term", scatter_dimension=1, tiled=True)
        return owned * valid

    first_sigma = apply_ham(first_vec)
    theta = lax.psum(jnp.sum(first_vec * first_sigma), ("term", "sector")) / total
    correction = (first_sigma - theta * first_vec) / jnp.maximum(jnp.abs(diagonal - theta), 1.0)
    correlation = lax.psum(jnp.sum(first_vec * correction), ("term", "sector")) / total
    orth = correction - correlation * first_vec
    orth_sq = lax.psum(jnp.sum(orth * orth), ("term", "sector")) / total
    new_vector = orth / jnp.sqrt(orth_sq + 1e-06)
    new_sigma = apply_ham(new_vector)
    upper, lower, corner = lax.psum(
        (
            jnp.sum(first_vec * new_sigma),
            jnp.sum(new_vector * first_sigma),
            jnp.sum(new_vector * new_sigma),
        ),
        ("term", "sector"),
    )
    subspace = jnp.stack(
        [jnp.stack([theta, upper / total]), jnp.stack([lower / total, corner / total])]
    )
    return (new_vector, new_sigma, subspace)


def solution(mesh):
    return jax.shard_map(
        local,
        mesh=mesh,
        in_specs=(
            P("sector", "term", None),
            P("term", "sector", None, None),
            P("term", "sector", None, None),
            P("sector", "term", None),
            P(),
            P("term", None),
        ),
        out_specs=(P("sector", "term", None), P("sector", "term", None), P()),
        check_vma=False,
    )
```

profile of v0, /device:TPU:1, one launch (start us, length us, event | category | flops | bytes accessed | tf_op | source)
XLA Modules:
  0.0 882.0 jit_solution(14392173964076206759)
XLA Ops:
  7.2 1.2 dynamic_slice.6
  8.5 0.6 iota_compare_fusion
  9.1 0.7 add_compare_fusion
  9.8 1.4 multiply_reduce_fusion.6
  11.2 81.4 %psum.49 = f32[]{:T(128)} all-reduce(f32[]{:T(128)} %multiply_reduce_fusion.6), channel_id=1, replica_groups=mesh['term'=32,'sector'=8] {'term','sector'}, use_global_device_ids=true, to_apply=%region_1.0 | all-reduce | flops 1 | bytes 8 | tf_op jit(solution)/shard_map/psum | solution.py:23
  93.3 0.8 fusion.50
  94.1 44.1 %all_gather.12 = bf16[1,512,512]{2,1,0:T(8,128)(2,1)} all-gather(bf16[1,16,512]{2,1,0:T(8,128)(2,1)S(1)} %fusion.50), channel_id=1, replica_groups=mesh['term'=32,'sector'=8] {'term'}, dimensions={1}, use_global_device_ids=true | all-gather | bytes 540672 | tf_op jit(solution)/shard_map/all_gather | solution.py:28
  138.2 0.0 reduce-scatter.3.cloned.1.call-start
  138.3 0.9 fusion.45
  139.2 0.9 and_reduce_fusion
  140.1 86.3 %all-gather.3.cloned.1.call-done = bf16[8,512,512]{2,1,0:T(8,128)(2,1)} async-done(((bf16[1,512,512]{2,1,0:T(8,128)(2,1)}), bf16[8,512,512]{2,1,0:T(8,128)(2,1)}) %all-gather.3.cloned.1.call-update) | async-done | bytes 4194320 | tf_op jit(solution)/shard_map/all_gather | solution.py:29
  226.3 5.0 gather_fusion
  231.3 10.3 %fusion.18 = f32[1,512,512]{2,1,0:T(8,128)} fusion(bf16[8,1,512,512]{3,2,1,0:T(8,128)(2,1)} %param.10, bf16[8,1,512,512]{3,2,1,0:T(8,128)(2,1)} %param.9, bf16[8,512,512]{2,1,0:T(8,128)(2,1)} %gather_fusion, pred[8]{0:T(512)(128)(4,1)S(1)} %and_reduce_fusion), kind=kOutput, calls=%fused_computation.22 | convolution fusion | flops 4299161600 | bytes 13631496 | tf_op jit(solution)/shard_map/tpij,tpkj->pik/dot_general | solution.py:35
  241.6 0.0 all-gather.5.cloned.1.call-start
  241.7 87.8 %reduce-scatter.3.cloned.1.call-done = f32[1,16,512]{2,1,0:T(8,128)} async-done(((f32[1,512,512]{2,1,0:T(8,128)}), f32[1,16,512]{2,1,0:T(8,128)}) %reduce-scatter.3.cloned.1.call-update) | async-done | bytes 32784 | tf_op jit(solution)/shard_map/reduce_scatter | solution.py:38
  329.5 1.4 multiply_reduce_fusion.5
  330.9 75.8 %psum.50 = f32[]{:T(128)} all-reduce(f32[]{:T(128)} %multiply_reduce_fusion.5), channel_id=1, replica_groups=mesh['term'=32,'sector'=8] {'term','sector'}, use_global_device_ids=true, to_apply=%region_4.6 | all-reduce | flops 1 | bytes 8 | tf_op jit(solution)/shard_map/psum | solution.py:42
  407.3 1.5 multiply_reduce_fusion.4
  408.8 73.4 %psum.51 = f32[]{:T(128)} all-reduce(f32[]{:T(128)} %get-tuple-element.13), channel_id=1, replica_groups=mesh['term'=32,'sector'=8] {'term','sector'}, use_global_device_ids=true, to_apply=%region_6.8 | all-reduce | flops 1 | bytes 8 | tf_op jit(solution)/shard_map/psum | solution.py:44
  482.8 0.7 multiply_reduce_fusion.3
  483.5 73.4 %psum.52 = f32[]{:T(128)} all-reduce(f32[]{:T(128)} %multiply_reduce_fusion.3), channel_id=1, replica_groups=mesh['term'=32,'sector'=8] {'term','sector'}, use_global_device_ids=true, to_apply=%region_8.10 | all-reduce | flops 1 | bytes 8 | tf_op jit(solution)/shard_map/psum | solution.py:46
  557.6 0.1 fusion.51
  557.7 46.8 %all_gather.14 = bf16[1,512,512]{2,1,0:T(8,128)(2,1)} all-gather(bf16[1,16,512]{2,1,0:T(8,128)(2,1)S(1)} %get-tuple-element.11), channel_id=1, replica_groups=mesh['term'=32,'sector'=8] {'term'}, dimensions={1}, use_global_device_ids=true | all-gather | bytes 540672 | tf_op jit(solution)/shard_map/all_gather | solution.py:28
  604.5 0.2 reduce-scatter.5.cloned.1.call-start
  604.7 87.0 %all-gather.5.cloned.1.call-done = bf16[8,512,512]{2,1,0:T(8,128)(2,1)} async-done(((bf16[1,512,512]{2,1,0:T(8,128)(2,1)}), bf16[8,512,512]{2,1,0:T(8,128)(2,1)}) %all-gather.5.cloned.1.call-update) | async-done | bytes 4194320 | tf_op jit(solution)/shard_map/all_gather | solution.py:29
  691.8 5.0 gather_fusion.1
  696.7 10.3 %fusion.23 = f32[1,512,512]{2,1,0:T(8,128)} fusion(bf16[8,1,512,512]{3,2,1,0:T(8,128)(2,1)} %param.10, bf16[8,512,512]{2,1,0:T(8,128)(2,1)} %gather_fusion.1, bf16[8,1,512,512]{3,2,1,0:T(8,128)(2,1)} %param.9, pred[8]{0:T(512)(128)(4,1)S(1)} %and_reduce_fusion), kind=kOutput, calls=%fused_computation.23 | convolution fusion | flops 4299161600 | bytes 13631496 | tf_op jit(solution)/shard_map/tpij,tpkj->pik/dot_general | solution.py:35
  707.0 87.9 %reduce-scatter.5.cloned.1.call-done = f32[1,16,512]{2,1,0:T(8,128)} async-done(((f32[1,512,512]{2,1,0:T(8,128)}), f32[1,16,512]{2,1,0:T(8,128)}) %reduce-scatter.5.cloned.1.call-update) | async-done | bytes 32784 | tf_op jit(solution)/shard_map/reduce_scatter | solution.py:38
  794.9 2.1 multiply_reduce_fusion.2
  797.0 76.0 %all-reduce = (f32[]{:T(128)}, f32[]{:T(128)}, f32[]{:T(128)}) all-reduce(f32[]{:T(128)} %get-tuple-element.5, f32[]{:T(128)} %get-tuple-element.6, f32[]{:T(128)} %get-tuple-element.4), channel_id=1, replica_groups=mesh['term'=32,'sector'=8] {'term','sector'}, use_global_device_ids=true, to_apply=%region_15.17 | all-reduce | flops 3 | bytes 24 | tf_op jit(solution)/shard_map/psum | solution.py:49
  874.9 0.1 maximum_bitcast_fusion
  874.9 0.6 pad_maximum_fusion
  (14 shorter events, 0.1 us)
Async XLA Ops:
  7.2 219.2 %all-gather.3.cloned.1.call-start = ((), (), s32[]{:S(2)}) async-start(), calls=%async_computation.2 | async-start | bytes 4718592 | tf_op jit(solution)/shard_map/all_gather | solution.py:29
  138.2 191.2 %reduce-scatter.3.cloned.1.call-start = ((), (), s32[]{:S(2)}) async-start(), calls=%async_computation.3 | async-start | bytes 1081344 | tf_op jit(solution)/shard_map/reduce_scatter | solution.py:38
  231.3 98.2 %copy-start = (f32[1,16,512]{2,1,0:T(8,128)S(1)}, f32[1,16,512]{2,1,0:T(8,128)}, u32[]{:S(2)}) copy-start(f32[1,16,512]{2,1,0:T(8,128)} %param.8) | copy-start | bytes 98308
  231.3 176.0 %copy-start.3 = (f32[1,16,512]{2,1,0:T(8,128)S(1)}, f32[1,16,512]{2,1,0:T(8,128)}, u32[]{:S(2)}) copy-start(f32[1,16,512]{2,1,0:T(8,128)} %param.11) | copy-start | bytes 98308
  241.6 450.2 %all-gather.5.cloned.1.call-start = ((), (), s32[]{:S(2)}) async-start(), calls=%async_computation.4 | async-start | bytes 4718592 | tf_op jit(solution)/shard_map/all_gather | solution.py:29
  557.7 237.2 %copy-start.2 = (f32[1,16,512]{2,1,0:T(8,128)}, f32[1,16,512]{2,1,0:T(8,128)S(1)}, u32[]{:S(2)}) copy-start(f32[1,16,512]{2,1,0:T(8,128)S(1)} %get-tuple-element.12) | copy-start | bytes 98308
  604.5 190.4 %reduce-scatter.5.cloned.1.call-start = ((), (), s32[]{:S(2)}) async-start(), calls=%async_computation.5 | async-start | bytes 1081344 | tf_op jit(solution)/shard_map/reduce_scatter | solution.py:38
  696.7 98.2 %copy-start.1 = (f32[1,16,512]{2,1,0:T(8,128)S(1)}, f32[1,16,512]{2,1,0:T(8,128)}, u32[]{:S(2)}) copy-start(f32[1,16,512]{2,1,0:T(8,128)} %reduce-scatter.3.cloned.1.call-done) | copy-start | bytes 98308
Sparse Core Ops, SparseCore 0:
  138.4 87.9 all-gather.2
  241.7 87.6 reduce-scatter.2
  604.6 87.1 all-gather.4
  707.1 87.6 reduce-scatter.4
where the time goes:
time: 883 us; the launch traced here: 882 us
  blocking collectives  471 us (53%)
  waiting for transfers between devices  349 us (40%)
  matrix products  20.5 us (2%)
  between operations  18.4 us (2%)
  other arithmetic  11.8 us (1%)
  local copies, waits for them, and re-layouts  11.2 us (1%)
    reduce_scatter x2, waiting for transfers between devices, apply_ham(): lax.psum_scatter(partial_sum, 'term', scatter_dimension=1, tiled=True)  176 us
    all_gather x2, waiting for transfers between devices, apply_ham(): every_block = lax.all_gather(blocks, 'sector', axis=0, tiled=True)  173 us
    all_gather x2, blocking collectives, apply_ham(): blocks = lax.all_gather(vector_b, 'term', axis=1, tiled=True)  90.9 us
    psum x1, blocking collectives, local(): squares = lax.psum(jnp.sum(masked * masked), ('term', 'sector'))  81.4 us
    psum x1, blocking collectives, local(): lax.psum((jnp.sum(first_vec * new_sigma), jnp.sum(new_vector * first_sigm...  76 us
    psum x1, blocking collectives, local(): lax.psum(jnp.sum(first_vec * first_sigma), ('term', 'sector')) / total  75.8 us
    psum x1, blocking collectives, local(): orth_sq = lax.psum(jnp.sum(orth * orth), ('term', 'sector')) / total  73.4 us
    psum x1, blocking collectives, local(): lax.psum(jnp.sum(first_vec * correction), ('term', 'sector')) / total  73.4 us
  transfers between devices with their start and end apart: 4, of which 4 were waited for; matrix products, arithmetic and copies ran while one was open for 0% of the time, Pallas kernels for 0%

commit v1 on v0

v1 whole, which is shorter than its diff:
```python
import jax
import jax.numpy as jnp
from jax import lax
from jax.experimental import pallas as pl
from jax.experimental.pallas import tpu as pltpu
from jax.sharding import PartitionSpec as P

MESH = pl.DeviceIdType.MESH
F32 = jnp.float32
BF16 = jnp.bfloat16

NX, NY, NZH, NZL, NC = 4, 4, 4, 2, 2
NZ = NZH * NZL

AG_FIRST = 0
AG_ZR = 3
AG_ZL = 7
AG_GR = 11
AG_GL = 19
AG_HR = 27
AG_HL = 35
AG_M = 43
RS_C = 75
RS = 76
AR1 = 92
AR2 = 100
AR3 = 104
NSEM = 112


def device(x, y, z, c):
    return {"term": (z // NZL) * (NX * NC) + x * NC + c, "sector": y * NZL + z % NZL}


def kernel(
    total,
    bs_ref,
    source_ref,
    wave_ref,
    diag_ref,
    left_hbm,
    right_hbm,
    vec_ref,
    sig_ref,
    sub_ref,
    left,
    right,
    v1,
    v2,
    acc,
    rs_core,
    rs_send,
    rs_recv,
    ar1,
    ar2,
    ar3,
    keep,
    send,
    recv,
    local_sem,
):
    term = lax.axis_index("term")
    sector = lax.axis_index("sector")
    c = term % NC
    x = (term // NC) % NX
    zh = term // (NX * NC)
    y = sector // NZL
    zl = sector % NZL
    z = zh * NZL + zl
    terms = left.shape[0]
    me = (x, y, z, c)

    def at(dx=0, dy=0, dz=0, dc=0):
        return device((x + dx) % NX, (y + dy) % NY, (z + dz) % NZ, (c + dc) % NC)

    def copy(src, dst, slot, dev):
        return pltpu.make_async_remote_copy(
            src_ref=src,
            dst_ref=dst,
            send_sem=send.at[slot],
            recv_sem=recv.at[slot],
            device_id=dev,
            device_id_type=MESH,
        )

    load_left = pltpu.make_async_copy(left_hbm.at[:, 0], left, local_sem.at[0])
    load_right = pltpu.make_async_copy(right_hbm.at[:, 0], right, local_sem.at[1])
    load_left.start()
    load_right.start()

    rows = term * 16 + lax.broadcasted_iota(jnp.int32, (16, 512), 0)
    cols = lax.broadcasted_iota(jnp.int32, (16, 512), 1)
    size = bs_ref[sector]
    valid = ((rows < size) & (cols < size)).astype(F32)
    masked = wave_ref[0] * valid
    keep[0] = masked
    v1[y, zl, zh, x, c] = masked.astype(BF16)

    barrier = pltpu.get_barrier_semaphore()
    peers = [at(dx=d) for d in (1, 2, 3)] + [at(dy=d) for d in (1, 2, 3)]
    peers += [at(dz=d) for d in (1, 7)] + [at(dc=1)]
    for dev in peers:
        pl.semaphore_signal(barrier, inc=1, device_id=dev, device_id_type=MESH)
    pl.semaphore_wait(barrier, len(peers))

    def gather(v, cs):
        if cs == 0:
            f, g = x, y

            def ref(gg, zz, ff):
                return v.at[gg, zz % NZL, zz // NZL, ff, 0]

            def dev_f(d):
                return at(dx=d)

            def dev_g(d):
                return at(dy=d)

        else:
            f, g = y, x

            def ref(gg, zz, ff):
                return v.at[ff, zz % NZL, zz // NZL, gg, 1]

            def dev_f(d):
                return at(dy=d)

            def dev_g(d):
                return at(dx=d)

        every, half_a, half_b = slice(None), pl.ds(0, 2), pl.ds(2, 2)
        sent = []
        mirrored = []

        def go(slot, gg, zz, ff, dev):
            cp = copy(ref(gg, zz, ff), ref(gg, zz, ff), slot, dev)
            cp.start()
            sent.append(cp)

        def got(slot, gg, zz, ff):
            copy(ref(gg, zz, ff), ref(gg, zz, ff), slot, at(dc=1)).wait_recv()

        def mirror(gg, zz):
            slot = AG_M + len(mirrored)
            mirrored.append((gg, zz))
            go(slot, gg, zz, every, at(dc=1))

        gi = lambda d: (g + d) % 4
        fi = lambda d: (f + d) % 4
        zi = lambda d: (z + d) % NZ

        for d in (2, 1, 3):
            go(AG_FIRST + d - 1, g, z, f, dev_f(d))
        for d in (1, 3, 2):
            got(AG_FIRST + d - 1, g, z, fi(-d))

        def g_send(b):
            zz = zi(b)
            go(AG_GR + b % 8, g, zz, every, dev_g(1))
            go(AG_GL + b % 8, g, zz, every, dev_g(-1))
            mirror(g, zz)

        def g_pass(b):
            zz = zi(b)
            got(AG_GR + b % 8, gi(-1), zz, every)
            go(AG_HR + b % 8, gi(-1), zz, half_a, dev_g(1))
            mirror(gi(-1), zz)
            got(AG_GL + b % 8, gi(1), zz, every)
            go(AG_HL + b % 8, gi(1), zz, half_b, dev_g(-1))
            mirror(gi(1), zz)

        def g_end(b):
            zz = zi(b)
            got(AG_HR + b % 8, gi(2), zz, half_a)
            got(AG_HL + b % 8, gi(2), zz, half_b)
            mirror(gi(2), zz)

        go(AG_ZR, g, z, every, at(dz=1))
        go(AG_ZL, g, z, every, at(dz=-1))
        g_send(0)
        for k in (1, 2, 3):
            got(AG_ZR + k - 1, g, zi(-k), every)
            go(AG_ZR + k, g, zi(-k), every if k < 3 else half_a, at(dz=1))
            got(AG_ZL + k - 1, g, zi(k), every)
            go(AG_ZL + k, g, zi(k), every if k < 3 else half_b, at(dz=-1))
            g_send(-k)
            g_send(k)
            if k == 1:
                g_pass(0)
            else:
                g_pass(1 - k)
                g_pass(k - 1)
        got(AG_ZR + 3, g, zi(4), half_a)
        got(AG_ZL + 3, g, zi(4), half_b)
        g_send(4)
        g_pass(-3)
        g_pass(3)
        for b in (0, -1, 1):
            g_end(b)
        g_pass(4)
        for b in (-2, 2, -3, 3, 4):
            g_end(b)
        for i in range(len(mirrored)):
            slot = AG_M + i
            copy(ref(g, z, every), ref(g, z, every), slot, at(dc=1)).wait_recv()
        for cp in sent:
            cp.wait_send()

    def all_gather(v):
        @pl.when(c == 0)
        def _():
            gather(v, 0)

        @pl.when(c == 1)
        def _():
            gather(v, 1)

    def apply_ops(v):
        acc[...] = jnp.zeros_like(acc)

        def step(t, carry):
            src = source_ref[t, sector]
            block = v[src >> 1, src & 1].reshape(512, 512)
            half = jnp.dot(left[t], block, preferred_element_type=F32).astype(BF16)
            part = lax.dot_general(
                half, right[t], (((1,), (1,)), ((), ())), preferred_element_type=F32
            )
            acc[...] += part.reshape(acc.shape)
            return carry

        lax.fori_loop(0, terms, step, 0)

    def row(p):
        p = jnp.sum(p.reshape(-1, 8, 512), axis=0)
        p = p[:, :128] + p[:, 128:256] + p[:, 256:384] + p[:, 384:]
        return jnp.sum(p, axis=0, keepdims=True)

    def inner(v):
        def step(i, carry):
            prod = v[y, zl, i].astype(F32) * acc[i]
            return carry + jnp.sum(prod.reshape(-1, 8, 512), axis=0)

        return row(lax.fori_loop(0, NZH, step, jnp.zeros((8, 512), F32)))

    def tile(parts):
        index = lax.broadcasted_iota(jnp.int32, (8, 128), 0)
        out = jnp.zeros((8, 128), F32)
        for i, p in enumerate(parts):
            out = jnp.where(index == i, jnp.broadcast_to(p, (8, 128)), out)
        return out

    def reduce_out(parts_of):
        core = copy(acc.at[:, :, 1 - c], rs_core, RS_C, at(dc=1))
        core.start()
        sent = [core]
        mine1 = x * NC + c
        ar1[mine1] = tile(parts_of())
        for d in range(1, 8):
            k = (mine1 + d) % 8
            dev = device(k // NC, y, z, k % NC)
            cp = copy(ar1.at[mine1], ar1.at[mine1], AR1 + d, dev)
            cp.start()
            sent.append(cp)
        core.wait_recv()
        rs_core[...] = acc[:, :, c] + rs_core[...]
        rs_send[...] = rs_core[...].astype(BF16)
        mine = zh * NX + x
        for dzh in (2, 1, 3, 0):
            for dx in (2, 1, 3, 0):
                if dzh == 0 and dx == 0:
                    continue
                slot = dzh * NX + dx
                zt = (zh + dzh) % NZH
                xt = (x + dx) % NX
                cp = copy(
                    rs_send.at[zt, xt],
                    rs_recv.at[slot],
                    RS + slot,
                    device(xt, y, zt * NZL + zl, c),
                )
                cp.start()
                sent.append(cp)
        for d in range(1, 8):
            k = (mine1 + 8 - d) % 8
            copy(ar1.at[k], ar1.at[k], AR1 + d, at(dc=1)).wait_recv()
        ar2[y] = jnp.sum(ar1[...], axis=0)
        for d in (2, 1, 3):
            cp = copy(ar2.at[y], ar2.at[y], AR2 + d, at(dy=d))
            cp.start()
            sent.append(cp)
        for d in (1, 3, 2):
            k = (y + 4 - d) % 4
            copy(ar2.at[k], ar2.at[k], AR2 + d, at(dc=1)).wait_recv()
        ar3[z] = jnp.sum(ar2[...], axis=0)
        for d in (4, 3, 5, 2, 6, 1, 7):
            cp = copy(ar3.at[z], ar3.at[z], AR3 + d, at(dz=d))
            cp.start()
            sent.append(cp)
        result = rs_core[zh, x]
        for dzh in (0, 1, 3, 2):
            for dx in (0, 1, 3, 2):
                slot = dzh * NX + dx
                if slot == 0:
                    continue
                copy(rs_recv.at[slot], rs_recv.at[slot], RS + slot, at(dc=1)).wait_recv()
                result = result + rs_recv[slot].astype(F32)
        for d in range(1, 8):
            k = (z + 8 - d) % 8
            copy(ar3.at[k], ar3.at[k], AR3 + d, at(dc=1)).wait_recv()
        sums = jnp.sum(ar3[...], axis=0)
        for cp in sent:
            cp.wait_send()
        return result * valid, sums

    def scalar(sums, i):
        return jnp.sum(sums[i : i + 1, :], axis=1, keepdims=True)

    all_gather(v1)
    load_left.wait()
    load_right.wait()
    apply_ops(v1)
    raw, sums = reduce_out(lambda: [row(keep[0] * keep[0]), inner(v1)])
    squares = scalar(sums, 0) / total
    scale = 1.0 / jnp.sqrt(squares + 1e-06)
    theta = scale * scale * scalar(sums, 1) / total
    first_vec = keep[0] * scale
    first_sigma = raw * scale
    correction = (first_sigma - theta * first_vec) / jnp.maximum(
        jnp.abs(diag_ref[0] - theta), 1.0
    )
    keep[1] = correction
    keep[2] = first_sigma
    keep[0] = first_vec
    v2[y, zl, zh, x, c] = correction.astype(BF16)

    all_gather(v2)
    apply_ops(v2)
    raw2, sums = reduce_out(
        lambda: [
            row(keep[0] * keep[1]),
            row(keep[1] * keep[1]),
            row(keep[1] * keep[2]),
            inner(v1) * scale,
            inner(v2),
        ]
    )
    first_sq = scale * scale * squares
    corre = scalar(sums, 0) / total
    corr_sq = scalar(sums, 1) / total
    corr_sigma = scalar(sums, 2) / total
    first_raw = scalar(sums, 3) / total
    corr_raw = scalar(sums, 4) / total
    orth_sq = jnp.maximum(corr_sq - 2.0 * corre * corre + corre * corre * first_sq, 0.0)
    norm = 1.0 / jnp.sqrt(orth_sq + 1e-06)
    vec_ref[0] = (keep[1] - corre * keep[0]) * norm
    sig_ref[0] = (raw2 - corre * keep[2]) * norm
    upper = (first_raw - corre * theta) * norm
    lower = (corr_sigma - corre * theta) * norm
    corner = (
        (corr_raw - corre * corr_sigma - corre * first_raw + corre * corre * theta)
        * norm
        * norm
    )
    r = lax.broadcasted_iota(jnp.int32, (2, 2), 0)
    q = lax.broadcasted_iota(jnp.int32, (2, 2), 1)
    low = jnp.where(q == 0, lower, corner)
    high = jnp.where(q == 0, theta, upper)
    sub_ref[...] = jnp.where(r == 0, high, low)


def local(wave, left_ops, right_ops, diagonal, block_size, source):
    terms, _, width, _ = left_ops.shape
    total = float(block_size.shape[0] * width * width)
    vmem = pl.BlockSpec(memory_space=pltpu.VMEM)
    smem = pl.BlockSpec(memory_space=pltpu.SMEM)
    hbm = pl.BlockSpec(memory_space=pl.ANY)
    slab = (16, width)

    def body(*refs):
        kernel(total, *refs)

    return pl.pallas_call(
        body,
        out_shape=(
            jax.ShapeDtypeStruct((1,) + slab, F32),
            jax.ShapeDtypeStruct((1,) + slab, F32),
            jax.ShapeDtypeStruct((2, 2), F32),
        ),
        in_specs=[smem, smem, vmem, vmem, hbm, hbm],
        out_specs=(vmem, vmem, vmem),
        scratch_shapes=[
            pltpu.VMEM((terms, width, width), BF16),
            pltpu.VMEM((terms, width, width), BF16),
            pltpu.VMEM((NY, NZL, NZH, NX, NC) + slab, BF16),
            pltpu.VMEM((NY, NZL, NZH, NX, NC) + slab, BF16),
            pltpu.VMEM((NZH, NX, NC) + slab, F32),
            pltpu.VMEM((NZH, NX) + slab, F32),
            pltpu.VMEM((NZH, NX) + slab, BF16),
            pltpu.VMEM((NZH * NX,) + slab, BF16),
            pltpu.VMEM((8, 8, 128), F32),
            pltpu.VMEM((4, 8, 128), F32),
            pltpu.VMEM((8, 8, 128), F32),
            pltpu.VMEM((3,) + slab, F32),
            pltpu.SemaphoreType.DMA((NSEM,)),
            pltpu.SemaphoreType.DMA((NSEM,)),
            pltpu.SemaphoreType.DMA((2,)),
        ],
        compiler_params=pltpu.CompilerParams(
            collective_id=0, has_side_effects=True, vmem_limit_bytes=48 * 1024 * 1024
        ),
    )(block_size, source, wave, diagonal, left_ops, right_ops)


def solution(mesh):
    return jax.shard_map(
        local,
        mesh=mesh,
        in_specs=(
            P("sector", "term", None),
            P("term", "sector", None, None),
            P("term", "sector", None, None),
            P("sector", "term", None),
            P(),
            P("term", None),
        ),
        out_specs=(P("sector", "term", None), P("sector", "term", None), P()),
        check_vma=False,
    )
```

time: 883 us -> 106 us (0.12)
  blocking collectives: 471 us -> 0 us
  waiting for transfers between devices: 349 us -> 0 us
  Pallas kernels: 0 us -> 98.6 us
  matrix products: 20.5 us -> 0 us
  between operations: 18.4 us -> 0.65 us
  other arithmetic: 11.8 us -> 0 us
    psum x5 -> x0, blocking collectives: 380 us -> none  [the longest x1 81.4 us: local(): squares = lax.psum(jnp.sum(masked * masked), ('term', 'sector'))]
    reduce_scatter x2 -> x0, waiting for transfers between devices: 176 us -> none  [apply_ham(): lax.psum_scatter(partial_sum, 'term', scatter_dimension=1, tiled=True)]
    all_gather x2 -> x0, waiting for transfers between devices: 173 us -> none  [apply_ham(): every_block = lax.all_gather(blocks, 'sector', axis=0, tiled=True)]
    pallas_call x0 -> x1, Pallas kernels: none -> 98.6 us  [local(): pl.pallas_call(body, out_shape=(jax.ShapeDtypeStruct((1,) + slab, F32), j...]
    all_gather x2 -> x0, blocking collectives: 90.9 us -> none  [apply_ham(): blocks = lax.all_gather(vector_b, 'term', axis=1, tiled=True)]
    dot_general x2 -> x0, matrix products: 20.5 us -> none  [apply_ham(): jnp.einsum('tpij,tpkj->pik', halfway_b, right_ops, preferred_element_type...]
    gather x2 -> x0, local copies, waits for them, and re-layouts: 9.94 us -> none  [apply_ham(): chosen = jnp.take(every_block, sources, axis=0)]
  transfers between devices with their start and end apart: 4 -> 0, of which waited for: 4 -> 0; matrix products, arithmetic and copies ran while one was open for 0% -> 0% of each run, Pallas kernels for 0% -> 0%
where the time goes in v1:
time: 106 us
  Pallas kernels  98.6 us (93%)
  local copies, waits for them, and re-layouts  6.83 us (6%)
    pallas_call x1, Pallas kernels, local(): pl.pallas_call(body, out_shape=(jax.ShapeDtypeStruct((1,) + slab, F32), j...  98.6 us
    unnamed x13, local copies, waits for them, and re-layouts  6.83 us

profile of v1, /device:TPU:1, one launch (start us, length us, event | category | flops | bytes accessed | tf_op | source)
XLA Modules:
  0.0 106.1 jit_solution(3923902739284367496)
XLA Ops:
  0.6 0.0 copy-start
  0.6 2.2 %copy-done = bf16[8,1,512,512]{3,2,1,0:T(8,128)(2,1)S(1)} copy-done((bf16[8,1,512,512]{3,2,1,0:T(8,128)(2,1)S(1)}, bf16[8,1,512,512]{3,2,1,0:T(8,128)(2,1)}, u32[]{:S(2)}) %copy-start) | copy-done | bytes 4194328
  2.8 0.0 copy-start.1
  2.8 0.8 copy-done.1
  3.6 0.0 copy-start.2
  3.6 0.8 copy-done.2
  4.3 0.0 copy-start.3
  4.3 0.7 copy-done.3
  5.0 0.0 copy-start.4
  5.0 0.7 copy-done.4
  5.7 98.6 %shard_map.85 = (f32[1,16,512]{2,1,0:T(8,128)S(1)}, f32[1,16,512]{2,1,0:T(8,128)S(1)}, f32[2,2]{1,0:T(2,128)S(1)}) custom-call(s32[8]{0:T(128)S(1)} %copy-done.4, s32[8,8]{1,0:T(8,128)S(1)} %copy-done.3, f32[1,16,512]{2,1,0:T(8,128)S(1)} %copy-done.1, f32[1,16,512]{2,1,0:T(8,128)S(1)} %copy-done.2, bf16[8,1,512,512]{3,2,1,0:T(8,128)(2,1)S(1)} %copy-done, ...), custom_call_target="tpu_custom_call" | custom-call | tf_op jit(solution)/shard_map/pallas_call | solution.py:382
  104.3 0.6 copy.12
  104.9 0.6 copy.13
  105.5 0.6 copy.14
Async XLA Ops:
  0.6 2.2 %copy-start = (bf16[8,1,512,512]{3,2,1,0:T(8,128)(2,1)S(1)}, bf16[8,1,512,512]{3,2,1,0:T(8,128)(2,1)}, u32[]{:S(2)}) copy-start(bf16[8,1,512,512]{3,2,1,0:T(8,128)(2,1)} %refs_4_.1) | copy-start | bytes 12582916
  2.8 0.8 copy-start.1
  3.6 0.8 copy-start.2
  4.3 0.7 copy-start.3
  5.0 0.7 copy-start.4

commit v2 on v1

v2 whole, which is shorter than its diff:
```python
import jax
import jax.numpy as jnp
from jax import lax
from jax.experimental import pallas as pl
from jax.experimental.pallas import tpu as pltpu
from jax.sharding import PartitionSpec as P

MESH = pl.DeviceIdType.MESH
F32 = jnp.float32
BF16 = jnp.bfloat16

NX, NY, NZH, NZL, NC = 4, 4, 4, 2, 2
NZ = NZH * NZL

TERMS_AT_ONCE = 2

AG_F2 = 0
AG_Z = 1
AG_Z2 = 8
AG_F = 15
AG_GR = 17
AG_GL = 21
AG_HR = 25
AG_HL = 29
AG_M = 33
RS_C = 49
RS = 50
AR1 = 66
AR2 = 82
NSEM = 98


def kernel(
    total,
    bs_hbm,
    source_hbm,
    wave_hbm,
    diag_hbm,
    left_hbm,
    right_hbm,
    vec_ref,
    sig_ref,
    sub_ref,
    bs_ref,
    source_ref,
    wave_ref,
    diag_ref,
    left,
    right,
    v1,
    v2,
    acc,
    rs_core,
    rs_send,
    rs_recv,
    ar1,
    ar2,
    keep,
    send,
    recv,
    local_sem,
):
    term = lax.axis_index("term")
    sector = lax.axis_index("sector")
    c = term % NC
    x = (term // NC) % NX
    zh = term // (NX * NC)
    y = sector // NZL
    zl = sector % NZL
    z = zh * NZL + zl
    terms = left.shape[0]

    xs = [x] + [(x + d) % NX for d in range(1, NX)]
    ys = [y] + [(y + d) % NY for d in range(1, NY)]
    zs = [z] + [(z + d) % NZ for d in range(1, NZ)]
    zhs = [zh] + [zz // NZL for zz in zs[1:]]
    zls = [zl, 1 - zl] * NZH
    cs_ = [c, 1 - c]

    def at(dx=0, dy=0, dz=0, dc=0):
        dx, dy, dz = dx % NX, dy % NY, dz % NZ
        return {
            "term": zhs[dz] * (NX * NC) + xs[dx] * NC + cs_[dc],
            "sector": ys[dy] * NZL + zls[dz],
        }

    def copy(src, dst, slot, dev):
        return pltpu.make_async_remote_copy(
            src_ref=src,
            dst_ref=dst,
            send_sem=send.at[slot],
            recv_sem=recv.at[slot],
            device_id=dev,
            device_id_type=MESH,
        )

    def load(src, dst, i):
        cp = pltpu.make_async_copy(src, dst, local_sem.at[i])
        cp.start()
        return cp

    barrier = pltpu.get_barrier_semaphore()
    peers = [at(dx=d) for d in (1, 2, 3)] + [at(dy=d) for d in (1, 2, 3)]
    peers += [at(dz=d) for d in range(1, NZ)] + [at(dc=1)]
    for dev in peers:
        pl.semaphore_signal(barrier, inc=1, device_id=dev, device_id_type=MESH)
    load_wave = load(wave_hbm, wave_ref, 0)
    load_bs = load(bs_hbm, bs_ref, 1)
    load_source = load(source_hbm, source_ref, 2)
    load_diag = load(diag_hbm, diag_ref, 3)
    load_left = load(left_hbm.at[:, 0], left, 4)
    load_right = load(right_hbm.at[:, 0], right, 5)

    load_bs.wait()
    load_wave.wait()
    rows = term * 16 + lax.broadcasted_iota(jnp.int32, (16, 512), 0)
    cols = lax.broadcasted_iota(jnp.int32, (16, 512), 1)
    size = bs_ref[sector]
    valid = ((rows < size) & (cols < size)).astype(F32)
    masked = wave_ref[0] * valid
    keep[0] = masked
    v1[y, zl, zh, x, c] = masked.astype(BF16)
    pl.semaphore_wait(barrier, len(peers))

    def gather(v, cs):
        fs, gs = (xs, ys) if cs == 0 else (ys, xs)
        every = slice(None)
        sent = []

        def piece(df, dz):
            i, j = (gs[0], fs[df % 4]) if cs == 0 else (fs[df % 4], gs[0])
            return v.at[i, zls[dz % NZ], zhs[dz % NZ], j, cs]

        def block(df, dg, part=every):
            i, j = (gs[dg % 4], fs[df % 4]) if cs == 0 else (fs[df % 4], gs[dg % 4])
            return v.at[i, :, part, j, cs]

        half_a, half_b = pl.ds(0, 2), pl.ds(2, 2)

        def dev_f(d):
            return at(dx=d) if cs == 0 else at(dy=d)

        def dev_g(d):
            return at(dy=d) if cs == 0 else at(dx=d)

        def go(slot, of, dev):
            copy(of(), of(), slot, dev).start()
            sent.append((slot, of))

        def got(slot, of):
            copy(of(), of(), slot, at(dc=1)).wait_recv()

        def mirror(df, dg):
            of = lambda: block(df, dg)
            go(AG_M + (df % 4) * 4 + dg % 4, of, at(dc=1))

        def g_send(df):
            go(AG_GR + df % 4, lambda: block(df, 0), dev_g(1))
            go(AG_GL + df % 4, lambda: block(df, 0), dev_g(-1))
            mirror(df, 0)

        def g_pass(df):
            got(AG_GR + df % 4, lambda: block(df, -1))
            go(AG_HR + df % 4, lambda: block(df, -1, half_a), dev_g(1))
            mirror(df, -1)
            got(AG_GL + df % 4, lambda: block(df, 1))
            go(AG_HL + df % 4, lambda: block(df, 1, half_b), dev_g(-1))
            mirror(df, 1)

        def g_end(df):
            got(AG_HR + df % 4, lambda: block(df, 2, half_a))
            got(AG_HL + df % 4, lambda: block(df, 2, half_b))
            mirror(df, 2)

        def z_send(df, slot):
            for d in (4, 3, 5, 2, 6, 1, 7):
                go(slot + d - 1, lambda: piece(df, 0), at(dz=d))

        def z_got(df, slot):
            for d in (1, 7, 2, 6, 3, 5, 4):
                got(slot + d - 1, lambda: piece(df, -d))

        def first():
            go(AG_F2, lambda: piece(0, 0), dev_f(2))
            z_send(0, AG_Z)

        def second():
            got(AG_F2, lambda: piece(2, 0))
            z_send(2, AG_Z2)

        def third():
            z_got(0, AG_Z)
            go(AG_F, lambda: block(0, 0), dev_f(1))
            go(AG_F + 1, lambda: block(0, 0), dev_f(-1))
            g_send(0)

        def fourth():
            z_got(2, AG_Z2)
            g_send(2)

        def fifth():
            got(AG_F, lambda: block(-1, 0))
            g_send(-1)
            got(AG_F + 1, lambda: block(1, 0))
            g_send(1)

        def pass_0():
            g_pass(0)

        def pass_2():
            g_pass(2)

        def pass_1():
            g_pass(-1)
            g_pass(1)

        def end_0():
            g_end(0)

        def end_2():
            g_end(2)

        def end_1():
            g_end(-1)
            g_end(1)

        def last():
            for i in range(16):
                got(AG_M + i, lambda: block(0, 0))

        def sent_all():
            for slot, of in sent:
                copy(of(), of(), slot, at(dc=1)).wait_send()

        arrive = [first, third, second, pass_0, fifth, fourth]
        arrive += [end_0, pass_1, pass_2, end_1, end_2, last]
        return arrive, sent_all

    def all_gather(v):
        steps = [gather(v, cs) for cs in range(NC)]

        def run(todo):
            for cs in range(NC):

                @pl.when(c == cs)
                def _(cs=cs):
                    for step in todo(*steps[cs]):
                        step()

        run(lambda arrive, sent_all: arrive)
        return lambda: run(lambda arrive, sent_all: [sent_all])

    def apply_ops(v):
        acc[...] = jnp.zeros_like(acc)

        def step(i, carry):
            halves, rights = [], []
            for k in range(TERMS_AT_ONCE):
                t = i * TERMS_AT_ONCE + k
                src = source_ref[t, sector]
                block = v[src >> 1, src & 1].reshape(512, 512)
                half = jnp.dot(left[t], block, preferred_element_type=F32)
                halves.append(half.astype(BF16))
                rights.append(right[t])
            part = lax.dot_general(
                jnp.concatenate(halves, axis=1),
                jnp.concatenate(rights, axis=1),
                (((1,), (1,)), ((), ())),
                preferred_element_type=F32,
            )
            acc[...] += part.reshape(acc.shape)
            return carry

        lax.fori_loop(0, terms // TERMS_AT_ONCE, step, 0)

    def row(p):
        p = jnp.sum(p.reshape(-1, 8, 512), axis=0)
        p = p[:, :128] + p[:, 128:256] + p[:, 256:384] + p[:, 384:]
        return jnp.sum(p, axis=0, keepdims=True)

    def inner(v):
        def step(i, carry):
            prod = v[y, zl, i].astype(F32) * acc[i]
            return carry + jnp.sum(prod.reshape(-1, 8, 512), axis=0)

        return row(lax.fori_loop(0, NZH, step, jnp.zeros((8, 512), F32)))

    def tile(parts):
        index = lax.broadcasted_iota(jnp.int32, (8, 128), 0)
        out = jnp.zeros((8, 128), F32)
        for i, p in enumerate(parts):
            out = jnp.where(index == i, jnp.broadcast_to(p, (8, 128)), out)
        return out

    def reduce_out(parts_of, left_to_wait):
        core = copy(acc.at[:, :, 1 - c], rs_core, RS_C, at(dc=1))
        core.start()
        sent = [core]
        ar1[z, c] = tile(parts_of())
        far = (4, 3, 5, 2, 6, 1, 7, 0)
        zc = [(dz, dc) for dz in far for dc in (0, 1) if dz or dc]
        xy = [(dx, dy) for dx in (2, 1, 3, 0) for dy in (2, 1, 3, 0) if dx or dy]
        for dz, dc in zc:
            cp = copy(ar1.at[z, c], ar1.at[z, c], AR1 + dz * NC + dc, at(dz=dz, dc=dc))
            cp.start()
            sent.append(cp)
        core.wait_recv()
        rs_core[...] = acc[:, :, c] + rs_core[...]
        rs_send[...] = rs_core[...].astype(BF16)
        zx = [(dzh, dx) for dzh in (2, 1, 3, 0) for dx in (2, 1, 3, 0) if dzh or dx]
        for dzh, dx in zx:
            slot = dzh * NX + dx
            cp = copy(
                rs_send.at[zhs[dzh * NZL], xs[dx]],
                rs_recv.at[slot],
                RS + slot,
                at(dx=dx, dz=dzh * NZL),
            )
            cp.start()
            sent.append(cp)
        for dz, dc in reversed(zc):
            other = ar1.at[zs[-dz % NZ], cs_[dc]]
            copy(other, other, AR1 + dz * NC + dc, at(dc=1)).wait_recv()
        ar2[x, y] = jnp.sum(ar1[...].reshape(NZ * NC, 8, 128), axis=0)
        for dx, dy in xy:
            cp = copy(ar2.at[x, y], ar2.at[x, y], AR2 + dx * NY + dy, at(dx=dx, dy=dy))
            cp.start()
            sent.append(cp)
        left_to_wait()
        result = rs_core[zh, x]
        for dzh, dx in reversed(zx):
            slot = dzh * NX + dx
            copy(rs_recv.at[slot], rs_recv.at[slot], RS + slot, at(dc=1)).wait_recv()
            result = result + rs_recv[slot].astype(F32)
        for dx, dy in reversed(xy):
            other = ar2.at[xs[-dx % NX], ys[-dy % NY]]
            copy(other, other, AR2 + dx * NY + dy, at(dc=1)).wait_recv()
        sums = jnp.sum(ar2[...].reshape(NX * NY, 8, 128), axis=0)

        def finish():
            for cp in sent:
                cp.wait_send()

        return result * valid, sums, finish

    def scalar(sums, i):
        return jnp.sum(sums[i : i + 1, :], axis=1, keepdims=True)

    left_to_wait = all_gather(v1)
    load_source.wait()
    load_left.wait()
    load_right.wait()
    apply_ops(v1)
    raw, sums, finish = reduce_out(
        lambda: [row(keep[0] * keep[0]), inner(v1)], left_to_wait
    )
    load_diag.wait()
    squares = scalar(sums, 0) / total
    scale = 1.0 / jnp.sqrt(squares + 1e-06)
    theta = scale * scale * scalar(sums, 1) / total
    first_vec = keep[0] * scale
    first_sigma = raw * scale
    correction = (first_sigma - theta * first_vec) / jnp.maximum(
        jnp.abs(diag_ref[0] - theta), 1.0
    )
    keep[1] = correction
    keep[2] = first_sigma
    keep[0] = first_vec
    v2[y, zl, zh, x, c] = correction.astype(BF16)

    left_to_wait = all_gather(v2)
    finish()
    apply_ops(v2)
    raw2, sums, finish = reduce_out(
        lambda: [
            row(keep[0] * keep[1]),
            row(keep[1] * keep[1]),
            row(keep[1] * keep[2]),
            inner(v1) * scale,
            inner(v2),
        ],
        left_to_wait,
    )
    first_sq = scale * scale * squares
    corre = scalar(sums, 0) / total
    corr_sq = scalar(sums, 1) / total
    corr_sigma = scalar(sums, 2) / total
    first_raw = scalar(sums, 3) / total
    corr_raw = scalar(sums, 4) / total
    orth_sq = jnp.maximum(corr_sq - 2.0 * corre * corre + corre * corre * first_sq, 0.0)
    norm = 1.0 / jnp.sqrt(orth_sq + 1e-06)
    vec_ref[0] = (keep[1] - corre * keep[0]) * norm
    sig_ref[0] = (raw2 - corre * keep[2]) * norm
    upper = (first_raw - corre * theta) * norm
    lower = (corr_sigma - corre * theta) * norm
    corner = (
        (corr_raw - corre * corr_sigma - corre * first_raw + corre * corre * theta)
        * norm
        * norm
    )
    r = lax.broadcasted_iota(jnp.int32, (2, 2), 0)
    q = lax.broadcasted_iota(jnp.int32, (2, 2), 1)
    low = jnp.where(q == 0, lower, corner)
    high = jnp.where(q == 0, theta, upper)
    sub_ref[...] = jnp.where(r == 0, high, low)
    finish()


def local(wave, left_ops, right_ops, diagonal, block_size, source):
    terms, _, width, _ = left_ops.shape
    total = float(block_size.shape[0] * width * width)
    vmem = pl.BlockSpec(memory_space=pltpu.VMEM)
    hbm = pl.BlockSpec(memory_space=pltpu.HBM)
    slab = (16, width)

    def body(*refs):
        kernel(total, *refs)

    return pl.pallas_call(
        body,
        out_shape=(
            jax.ShapeDtypeStruct((1,) + slab, F32),
            jax.ShapeDtypeStruct((1,) + slab, F32),
            jax.ShapeDtypeStruct((2, 2), F32),
        ),
        in_specs=[hbm] * 6,
        out_specs=(vmem, vmem, vmem),
        scratch_shapes=[
            pltpu.SMEM(block_size.shape, jnp.int32),
            pltpu.SMEM(source.shape, jnp.int32),
            pltpu.VMEM((1,) + slab, F32),
            pltpu.VMEM((1,) + slab, F32),
            pltpu.VMEM((terms, width, width), BF16),
            pltpu.VMEM((terms, width, width), BF16),
            pltpu.VMEM((NY, NZL, NZH, NX, NC) + slab, BF16),
            pltpu.VMEM((NY, NZL, NZH, NX, NC) + slab, BF16),
            pltpu.VMEM((NZH, NX, NC) + slab, F32),
            pltpu.VMEM((NZH, NX) + slab, F32),
            pltpu.VMEM((NZH, NX) + slab, BF16),
            pltpu.VMEM((NZH * NX,) + slab, BF16),
            pltpu.VMEM((NZ, NC, 8, 128), F32),
            pltpu.VMEM((NX, NY, 8, 128), F32),
            pltpu.VMEM((3,) + slab, F32),
            pltpu.SemaphoreType.DMA((NSEM,)),
            pltpu.SemaphoreType.DMA((NSEM,)),
            pltpu.SemaphoreType.DMA((6,)),
        ],
        compiler_params=pltpu.CompilerParams(
            collective_id=0, has_side_effects=True, vmem_limit_bytes=60 * 1024 * 1024
        ),
    )(block_size, source, wave, diagonal, left_ops, right_ops)


def solution(mesh):
    return jax.shard_map(
        local,
        mesh=mesh,
        in_specs=(
            P("sector", "term", None),
            P("term", "sector", None, None),
            P("term", "sector", None, None),
            P("sector", "term", None),
            P(),
            P("term", None),
        ),
        out_specs=(P("sector", "term", None), P("sector", "term", None), P()),
        check_vma=False,
    )
```

time: 106 us -> 92.9 us (0.88)
  Pallas kernels: 98.6 us -> 88.1 us
  local copies, waits for them, and re-layouts: 6.83 us -> 3.95 us
    pallas_call x1, Pallas kernels: 98.6 us -> 88.1 us  [local(): pl.pallas_call(body, out_shape=(jax.ShapeDtypeStruct((1,) + slab, F32), j...]
    unnamed x13 -> x3, local copies, waits for them, and re-layouts: 6.83 us -> 3.95 us
where the time goes in v2:
time: 92.9 us; the launch traced here: 92.6 us
  Pallas kernels  88.1 us (95%)
  local copies, waits for them, and re-layouts  3.95 us (4%)
    pallas_call x1, Pallas kernels, local(): pl.pallas_call(body, out_shape=(jax.ShapeDtypeStruct((1,) + slab, F32), j...  88.1 us
    unnamed x3, local copies, waits for them, and re-layouts  3.95 us

profile of v2, /device:TPU:1, one launch (start us, length us, event | category | flops | bytes accessed | tf_op | source)
XLA Modules:
  0.0 92.6 jit_solution(11822227069044131358)
XLA Ops:
  0.6 88.1 %shard_map.85 = (f32[1,16,512]{2,1,0:T(8,128)}, f32[1,16,512]{2,1,0:T(8,128)}, f32[2,2]{1,0:T(2,128)}) custom-call(s32[8]{0:T(128)} %refs_0_.1, s32[8,8]{1,0:T(8,128)} %refs_1_.1, f32[1,16,512]{2,1,0:T(8,128)} %refs_2_.1, f32[1,16,512]{2,1,0:T(8,128)} %refs_3_.1, bf16[8,1,512,512]{3,2,1,0:T(8,128)(2,1)} %refs_4_.1, bf16[8,1,512,512]{3,2,1,0:T(8,128)(2,1)} %refs_5_.1), custom_call_target="tpu_custom_call" | custom-call | tf_op jit(solution)/shard_map/pallas_call | solution.py:419
  88.7 1.4 %copy.12 = f32[1,16,512]{2,1,0:T(8,128)} copy(f32[1,16,512]{2,1,0:T(8,128)} %get-tuple-element.6) | data formatting | bytes 65536
  90.1 1.4 %copy.13 = f32[1,16,512]{2,1,0:T(8,128)} copy(f32[1,16,512]{2,1,0:T(8,128)} %get-tuple-element.7) | data formatting | bytes 65536
  91.4 1.2 %copy.14 = f32[2,2]{1,0:T(2,128)} copy(f32[2,2]{1,0:T(2,128)} %get-tuple-element.8) | data formatting | bytes 32

commit v3 on v2

--- a/solution.py
+++ b/solution.py
@@ -12,7 +12,7 @@
 NX, NY, NZH, NZL, NC = 4, 4, 4, 2, 2
 NZ = NZH * NZL
 
-TERMS_AT_ONCE = 2
+TERMS_AT_ONCE = 4
 
 AG_F2 = 0
 AG_Z = 1
@@ -416,7 +416,7 @@
     def body(*refs):
         kernel(total, *refs)
 
-    return pl.pallas_call(
+    vec, sig, sub = pl.pallas_call(
         body,
         out_shape=(
             jax.ShapeDtypeStruct((1,) + slab, F32),
@@ -450,6 +450,22 @@
         ),
     )(block_size, source, wave, diagonal, left_ops, right_ops)
 
+    def hand_out(vec_in, sig_in, sub_in, vec_out, sig_out, sub_out):
+        vec_out[...] = vec_in[...]
+        sig_out[...] = sig_in[...]
+        sub_out[...] = sub_in[...]
+
+    return pl.pallas_call(
+        hand_out,
+        out_shape=(
+            jax.ShapeDtypeStruct(vec.shape, F32),
+            jax.ShapeDtypeStruct(sig.shape, F32),
+            jax.ShapeDtypeStruct(sub.shape, F32),
+        ),
+        in_specs=[vmem] * 3,
+        out_specs=(vmem,) * 3,
+    )(vec, sig, sub)
+
 
 def solution(mesh):
     return jax.shard_map(

time: 92.9 us -> 89.6 us (0.964)
  local copies, waits for them, and re-layouts: 3.95 us -> 0 us
    unnamed x3 -> x0, local copies, waits for them, and re-layouts: 3.95 us -> none
    pallas_call x0 -> x1, Pallas kernels: none -> 1.41 us  [local(): pl.pallas_call(hand_out, out_shape=(jax.ShapeDtypeStruct(vec.shape, F32),...]
where the time goes in v3:
time: 89.6 us; the launch traced here: 89.4 us
  Pallas kernels  88.8 us (99%)
    pallas_call x1, Pallas kernels, local(): pl.pallas_call(body, out_shape=(jax.ShapeDtypeStruct((1,) + slab, F32), j...  87.4 us

profile of v3, /device:TPU:1, one launch (start us, length us, event | category | flops | bytes accessed | tf_op | source)
XLA Modules:
  0.0 89.4 jit_solution(18141690227366410120)
XLA Ops:
  0.6 87.4 %shard_map.85 = (f32[1,16,512]{2,1,0:T(8,128)}, f32[1,16,512]{2,1,0:T(8,128)}, f32[2,2]{1,0:T(2,128)}) custom-call(s32[8]{0:T(128)} %refs_0_.1, s32[8,8]{1,0:T(8,128)} %refs_1_.1, f32[1,16,512]{2,1,0:T(8,128)} %refs_2_.1, f32[1,16,512]{2,1,0:T(8,128)} %refs_3_.1, bf16[8,1,512,512]{3,2,1,0:T(8,128)(2,1)} %refs_4_.1, bf16[8,1,512,512]{3,2,1,0:T(8,128)(2,1)} %refs_5_.1), custom_call_target="tpu_custom_call" | custom-call | tf_op jit(solution)/shard_map/pallas_call | solution.py:419
  88.0 1.4 %shard_map.86 = (f32[1,16,512]{2,1,0:T(8,128)}, f32[1,16,512]{2,1,0:T(8,128)}, f32[2,2]{1,0:T(2,128)}) custom-call(f32[1,16,512]{2,1,0:T(8,128)} %get-tuple-element.6.vec_in, f32[1,16,512]{2,1,0:T(8,128)} %get-tuple-element.7.sig_in, f32[2,2]{1,0:T(2,128)} %get-tuple-element.8.sub_in), custom_call_target="tpu_custom_call" | custom-call | tf_op jit(solution)/shard_map/pallas_call | solution.py:458

commit v4 on v3

--- a/solution.py
+++ b/solution.py
@@ -12,7 +12,7 @@
 NX, NY, NZH, NZL, NC = 4, 4, 4, 2, 2
 NZ = NZH * NZL
 
-TERMS_AT_ONCE = 4
+TERMS_AT_ONCE = 8
 
 AG_F2 = 0
 AG_Z = 1

time: 89.6 us -> 89.2 us (level)
  no operation moved by 1% of the time
where the time goes in v4:
time: 89.2 us; the launch traced here: 89.1 us
  Pallas kernels  88.4 us (99%)
    pallas_call x1, Pallas kernels, local(): pl.pallas_call(body, out_shape=(jax.ShapeDtypeStruct((1,) + slab, F32), j...  87 us

profile of v4, /device:TPU:1, one launch (start us, length us, event | category | flops | bytes accessed | tf_op | source)
XLA Modules:
  0.0 89.1 jit_solution(17155147722823976603)
XLA Ops:
  0.6 87.0 %shard_map.85 = (f32[1,16,512]{2,1,0:T(8,128)}, f32[1,16,512]{2,1,0:T(8,128)}, f32[2,2]{1,0:T(2,128)}) custom-call(s32[8]{0:T(128)} %refs_0_.1, s32[8,8]{1,0:T(8,128)} %refs_1_.1, f32[1,16,512]{2,1,0:T(8,128)} %refs_2_.1, f32[1,16,512]{2,1,0:T(8,128)} %refs_3_.1, bf16[8,1,512,512]{3,2,1,0:T(8,128)(2,1)} %refs_4_.1, bf16[8,1,512,512]{3,2,1,0:T(8,128)(2,1)} %refs_5_.1), custom_call_target="tpu_custom_call" | custom-call | tf_op jit(solution)/shard_map/pallas_call | solution.py:419
  87.7 1.4 %shard_map.86 = (f32[1,16,512]{2,1,0:T(8,128)}, f32[1,16,512]{2,1,0:T(8,128)}, f32[2,2]{1,0:T(2,128)}) custom-call(f32[1,16,512]{2,1,0:T(8,128)} %get-tuple-element.6.vec_in, f32[1,16,512]{2,1,0:T(8,128)} %get-tuple-element.7.sig_in, f32[2,2]{1,0:T(2,128)} %get-tuple-element.8.sub_in), custom_call_target="tpu_custom_call" | custom-call | tf_op jit(solution)/shard_map/pallas_call | solution.py:458
